TPU v7x, 256 devices: a whole 4x4x8 slice. The times are simulated.
256 devices in a mesh: dp: 32 (over y_hi, z, core), shard: 8 (over x, y_lo).
Axes of the slice: x: 4, y: 4 (y_hi: 2, y_lo: 2; y = y_hi * 2 + y_lo), z: 8, core: 2. Of those that a mesh axis runs over, the one named last changes fastest.
Arguments:
- resid_in: bfloat16 [4096, 8192], P('dp', 'shard'), may hold values from -6 to 6
- hidden: bfloat16 [4096, 28672], P('shard', 'dp'), may hold values from -6 to 6
- w_down: bfloat16 [28672, 8192], P('dp', 'shard'), may hold values from -0.03125 to 0.03125
- frozen: bfloat16 [4096, 8192], P(('dp', 'shard')), may hold values from -6 to 6
- steer: bfloat16 [8192], P('shard'), may hold values from -6 to 6
- forget_flags: int32 [16], replicated, may hold values from 0 to 1, as said below
Outputs:
- updated: bfloat16 [4096, 8192], P('dp', 'shard')
- grad_down: float32 [28672, 8192], P('dp', 'shard')
Inputs may be any that keep to these rules, and one draw needn't show every extreme that they name: `forget_flags`: exactly half of the 16 sequences are forget sequences.
All inputs are finite; a program needn't handle non-finite values.
Results may differ from a plain program's by a relative error of at most 0.0019.
Values may be sent and summed in bfloat16 or wider, within the bound.
A program may use at most 128 MiB of HBM per device.

v0:
```python
import math
import jax
import jax.numpy as jnp
from jax import lax
from jax.sharding import PartitionSpec as P

SEQ_LEN = 256
retain_weight = 2.0


def per_device(resid_in, hidden, w_down, frozen, steer, forget_flags):
    whole_hidden = lax.all_gather(hidden, "shard", axis=0, tiled=True)
    tok_rows = resid_in.shape[0]
    mlp_out = lax.psum_scatter(
        jnp.dot(whole_hidden, w_down, preferred_element_type=jnp.float32),
        "dp",
        scatter_dimension=0,
        tiled=True,
    )
    residual = resid_in.astype(jnp.float32) + mlp_out
    updated = residual.astype(jnp.bfloat16)
    target_rows = lax.all_to_all(frozen, "shard", split_axis=1, concat_axis=0, tiled=True)
    start_row = lax.axis_index("dp") * tok_rows
    seq_ids = (start_row + jnp.arange(tok_rows, dtype=jnp.int32)) // SEQ_LEN
    seq_match = seq_ids[:, None] == jnp.arange(forget_flags.shape[0], dtype=jnp.int32)[None, :]
    is_forget = jnp.sum(jnp.where(seq_match, forget_flags[None, :], 0), axis=1) > 0
    total_tokens = tok_rows * lax.axis_size("dp")
    target = jnp.where(
        is_forget[:, None], steer.astype(jnp.float32)[None, :], target_rows.astype(jnp.float32)
    )
    loss_weight = jnp.where(is_forget, 1.0, retain_weight).astype(jnp.float32)
    slopes = (loss_weight[:, None] * (residual - target) * (1.0 / math.sqrt(total_tokens))).astype(
        jnp.bfloat16
    )
    all_slopes = lax.all_gather(slopes, "dp", axis=0, tiled=True)
    grad_down = lax.dot_general(
        whole_hidden, all_slopes, (((0,), (0,)), ((), ())), preferred_element_type=jnp.float32
    )
    return (updated, grad_down)


def solution(mesh):
    in_specs = (
        P("dp", "shard"),
        P("shard", "dp"),
        P("dp", "shard"),
        P(("dp", "shard"), None),
        P("shard"),
        P(),
    )
    out_specs = (P("dp", "shard"), P("dp", "shard"))
    return jax.shard_map(
        per_device, mesh=mesh, in_specs=in_specs, out_specs=out_specs, check_vma=False
    )
```

profile of v0, /device:TPU:1, one launch (start us, length us, event | category | flops | bytes accessed | tf_op | source)
XLA Modules:
  0.0 531.7 jit_solution(17514021398669694060)
XLA Ops:
  7.2 0.0 copy-start
  7.2 0.0 all-gather.3.cloned.1.call-start
  7.2 0.7 all-gather.3.cloned.1.call-update
  7.9 0.0 reduce-scatter.2.cloned.1.call-start
  8.0 156.9 %all-gather.3.cloned.1.call-done = bf16[4096,896]{1,0:T(8,128)(2,1)} async-done(((bf16[512,896]{1,0:T(8,128)(2,1)}), bf16[4096,896]{1,0:T(8,128)(2,1)}) %all-gather.3.cloned.1.call-update) | async-done | bytes 7340048 | tf_op jit(solution)/shard_map/all_gather | solution.py:12
  164.9 0.0 copy-done
  164.9 14.3 %fusion.5 = f32[4096,1024]{1,0:T(8,128)} fusion(bf16[4096,896]{1,0:T(8,128)(2,1)} %all-gather.3.cloned.1.call-done, bf16[896,1024]{1,0:T(8,128)(2,1)S(1)} %copy-done), kind=kOutput, calls=%fused_computation.17 | convolution fusion | flops 7516192768 | bytes 25952256 | tf_op jit(solution)/shard_map/dot_general | solution.py:15
  179.2 0.0 copy-start.1
  179.2 0.0 reduce-scatter.2.cloned.1.call-update
  179.3 0.9 copy-done.1
  180.2 0.7 copy.14
  180.9 7.4 %all-to-all-start = ((bf16[16,8,1024]{2,0,1:T(8,128)(2,1)}), bf16[16,8,1024]{2,0,1:T(8,128)(2,1)S(1)}, u32[]{:S(2)}, u32[]{:S(2)}) async-start(bf16[16,8,1024]{2,0,1:T(8,128)(2,1)} %bitcast.21), calls=%async_computation.1 | async-start | bytes 524288 | tf_op jit(solution)/shard_map/all_to_all | solution.py:22
  188.2 0.0 all-gather.5.cloned.1.call-start
  188.3 0.0 copy-done.4
  188.3 0.1 select_reduce_fusion
  188.4 0.0 copy-done.3
  188.4 5.7 %all-to-all-done = bf16[16,8,1024]{2,0,1:T(8,128)(2,1)S(1)} async-done(((bf16[16,8,1024]{2,0,1:T(8,128)(2,1)}), bf16[16,8,1024]{2,0,1:T(8,128)(2,1)S(1)}, u32[]{:S(2)}, u32[]{:S(2)}) %all-to-all-start) | async-done | bytes 262176 | tf_op jit(solution)/shard_map/all_to_all | solution.py:22
  194.2 203.4 %reduce-scatter.2.cloned.1.call-done = f32[128,1024]{1,0:T(8,128)} async-done(((f32[4096,1024]{1,0:T(8,128)}), f32[128,1024]{1,0:T(8,128)}) %reduce-scatter.2.cloned.1.call-update) | async-done | bytes 524304 | tf_op jit(solution)/shard_map/reduce_scatter | solution.py:14
  397.6 0.0 copy-done.2
  397.6 2.0 fusion.3
  399.6 0.0 all-gather.5.cloned.1.call-update
  399.6 105.9 %all-gather.5.cloned.1.call-done = bf16[4096,1024]{1,0:T(8,128)(2,1)} async-done(((bf16[128,1024]{1,0:T(8,128)(2,1)}), bf16[4096,1024]{1,0:T(8,128)(2,1)}) %all-gather.5.cloned.1.call-update) | async-done | bytes 8388624 | tf_op jit(solution)/shard_map/all_gather | solution.py:35
  505.6 14.6 %convolution_bitcast_fusion = f32[896,1024]{0,1:T(8,128)} fusion(bf16[4096,1024]{1,0:T(8,128)(2,1)} %all-gather.5.cloned.1.call-done, bf16[4096,896]{1,0:T(8,128)(2,1)} %all-gather.3.cloned.1.call-done), kind=kOutput, calls=%fused_computation | convolution fusion | flops 7516192768 | bytes 19398656 | tf_op jit(solution)/shard_map/dot_general | solution.py:36
  520.2 5.0 copy.11
  (7 shorter events, 0.0 us)
Async XLA Ops:
  7.2 157.7 %copy-start = (bf16[896,1024]{1,0:T(8,128)(2,1)S(1)}, bf16[896,1024]{1,0:T(8,128)(2,1)}, u32[]{:S(2)}) copy-start(bf16[896,1024]{1,0:T(8,128)(2,1)} %param.8) | copy-start | bytes 5505028
  7.2 157.7 %all-gather.3.cloned.1.call-start = ((), (), s32[]{:S(2)}) async-start(), calls=%async_computation.2 | async-start | bytes 8257536 | tf_op jit(solution)/shard_map/all_gather | solution.py:12
  7.9 389.7 %reduce-scatter.2.cloned.1.call-start = ((), (), s32[]{:S(2)}) async-start(), calls=%async_computation.3 | async-start | bytes 17301504 | tf_op jit(solution)/shard_map/reduce_scatter | solution.py:14
  179.2 0.9 copy-start.1
  179.2 9.1 %copy-start.4 = (s32[16]{0:T(128)S(1)}, s32[16]{0:T(128)}, u32[]{:S(2)}) copy-start(s32[16]{0:T(128)} %param.11) | copy-start | bytes 196
  179.2 9.2 %copy-start.3 = (bf16[1024]{0:T(1024)(128)(2,1)S(1)}, bf16[1024]{0:T(1024)(128)(2,1)}, u32[]{:S(2)}) copy-start(bf16[1024]{0:T(1024)(128)(2,1)} %param.10) | copy-start | bytes 6148
  179.2 218.4 %copy-start.2 = (bf16[128,1024]{1,0:T(8,128)(2,1)S(1)}, bf16[128,1024]{1,0:T(8,128)(2,1)}, u32[]{:S(2)}) copy-start(bf16[128,1024]{1,0:T(8,128)(2,1)} %param.6) | copy-start | bytes 786436
  180.9 13.3 %all-to-all-start = ((bf16[16,8,1024]{2,0,1:T(8,128)(2,1)}), bf16[16,8,1024]{2,0,1:T(8,128)(2,1)S(1)}, u32[]{:S(2)}, u32[]{:S(2)}) async-start(bf16[16,8,1024]{2,0,1:T(8,128)(2,1)} %bitcast.21), calls=%async_computation.1 | async-start | bytes 524288 | tf_op jit(solution)/shard_map/all_to_all | solution.py:22
  188.2 317.3 %all-gather.5.cloned.1.call-start = ((), (), s32[]{:S(2)}) async-start(), calls=%async_computation.4 | async-start | bytes 8650752 | tf_op jit(solution)/shard_map/all_gather | solution.py:35
Sparse Core Ops, SparseCore 0:
  9.8 155.0 all-gather.2
  179.4 218.1 reduce-scatter.1
  401.3 104.1 all-gather.4
where the time goes:
time: 532 us
  waiting for transfers between devices  473 us (89%)
  matrix products  29 us (5%)
  between operations  13.8 us (3%)
  starting transfers between devices  7.47 us (1%)
  local copies, waits for them, and re-layouts  6.64 us (1%)
    reduce_scatter x1, waiting for transfers between devices, per_device(): lax.psum_scatter(jnp.dot(whole_hidden, w_down, preferred_element_type=jnp...  203 us
    all_gather x1, waiting for transfers between devices, per_device(): whole_hidden = lax.all_gather(hidden, 'shard', axis=0, tiled=True)  157 us
    all_gather x1, waiting for transfers between devices, per_device(): all_slopes = lax.all_gather(slopes, 'dp', axis=0, tiled=True)  106 us
    dot_general x1, matrix products, per_device(): lax.dot_general(whole_hidden, all_slopes, (((0,), (0,)), ((), ())), prefe...  14.6 us
    dot_general x1, matrix products, per_device(): jnp.dot(whole_hidden, w_down, preferred_element_type=jnp.float32)  14.3 us
  transfers between devices with their start and end apart: 4, of which 4 were waited for; matrix products, arithmetic and copies ran while one was open for 0% of the time, Pallas kernels for 0%

commit v1 on v0

--- a/solution.py
+++ b/solution.py
@@ -9,7 +9,9 @@
 
 
 def per_device(resid_in, hidden, w_down, frozen, steer, forget_flags):
-    whole_hidden = lax.all_gather(hidden, "shard", axis=0, tiled=True)
+    whole_hidden = jnp.concatenate(
+        lax.all_to_all(jnp.stack([hidden] * lax.axis_size("shard")), "shard", 0, 0), axis=0
+    )
     tok_rows = resid_in.shape[0]
     mlp_out = lax.psum_scatter(
         jnp.dot(whole_hidden, w_down, preferred_element_type=jnp.float32),

time: 532 us -> 466 us (0.88)
  waiting for transfers between devices: 473 us -> 320 us
  blocking collectives: 0 us -> 88.4 us
    all_gather x1 -> x0, waiting for transfers between devices: 157 us -> none  [per_device(): whole_hidden = lax.all_gather(hidden, 'shard', axis=0, tiled=True)]
    all_to_all x0 -> x1, blocking collectives: none -> 88.4 us  [per_device(): lax.all_to_all(jnp.stack([hidden] * lax.axis_size('shard')), 'shard', 0, 0)]
  transfers between devices with their start and end apart: 4 -> 3, of which waited for: 4 -> 3; matrix products, arithmetic and copies ran while one was open for 0% -> 0% of each run, Pallas kernels for 0% -> 0%
where the time goes in v1:
time: 466 us
  waiting for transfers between devices  320 us (69%)
  blocking collectives  88.4 us (19%)
  matrix products  26.3 us (6%)
  between operations  14.1 us (3%)
  local copies, waits for them, and re-layouts  11.8 us (3%)
    reduce_scatter x1, waiting for transfers between devices, per_device(): lax.psum_scatter(jnp.dot(whole_hidden, w_down, preferred_element_type=jnp...  208 us
    all_gather x1, waiting for transfers between devices, per_device(): all_slopes = lax.all_gather(slopes, 'dp', axis=0, tiled=True)  106 us
    all_to_all x1, blocking collectives, per_device(): lax.all_to_all(jnp.stack([hidden] * lax.axis_size('shard')), 'shard', 0, 0)  88.4 us
    dot_general x1, matrix products, per_device(): lax.dot_general(whole_hidden, all_slopes, (((0,), (0,)), ((), ())), prefe...  14.6 us
    dot_general x1, matrix products, per_device(): jnp.dot(whole_hidden, w_down, preferred_element_type=jnp.float32)  11.7 us
  transfers between devices with their start and end apart: 3, of which 3 were waited for; matrix products, arithmetic and copies ran while one was open for 0% of the time, Pallas kernels for 0%

profile of v1, /device:TPU:1, one launch (start us, length us, event | category | flops | bytes accessed | tf_op | source)
XLA Modules:
  0.0 465.8 jit_solution(6009387594556144117)
XLA Ops:
  7.2 0.0 copy-start
  7.2 0.0 reduce-scatter.2.cloned.1.call-start
  7.2 2.2 stack.2
  9.5 88.4 %all_to_all.18 = bf16[8,512,896]{2,1,0:T(8,128)(2,1)S(1)} all-to-all(bf16[8,512,896]{2,1,0:T(8,128)(2,1)S(1)} %stack.2), channel_id=1, replica_groups=mesh['dp'=32,'shard'=8] {'shard'}, dimensions={0} | all-to-all | bytes 14680064 | tf_op jit(solution)/shard_map/all_to_all | solution.py:13
  97.9 0.0 copy-start.1
  97.9 2.9 copy-done.1
  100.8 0.0 copy-done
  100.8 11.7 %fusion.5 = f32[4096,1024]{1,0:T(8,128)} fusion(bf16[4096,896]{1,0:T(8,128)(2,1)S(1)} %bitcast.23, bf16[896,1024]{1,0:T(8,128)(2,1)S(1)} %copy-done), kind=kOutput, calls=%fused_computation.17 | convolution fusion | flops 7516192768 | bytes 25952256 | tf_op jit(solution)/shard_map/dot_general | solution.py:17
  112.5 0.0 reduce-scatter.2.cloned.1.call-update
  112.5 0.9 copy-done.2
  113.4 0.7 copy.14
  114.2 3.4 all-to-all-start.1
  117.6 0.0 all-gather.2.cloned.1.call-start
  117.7 0.0 copy-done.5
  117.7 0.1 select_reduce_fusion
  117.8 0.0 copy-done.4
  117.8 5.6 %all-to-all-done.1 = bf16[16,8,1024]{2,0,1:T(8,128)(2,1)S(1)} async-done(((bf16[16,8,1024]{2,0,1:T(8,128)(2,1)}), bf16[16,8,1024]{2,0,1:T(8,128)(2,1)S(1)}, u32[]{:S(2)}, u32[]{:S(2)}) %all-to-all-start.1) | async-done | bytes 262176 | tf_op jit(solution)/shard_map/all_to_all | solution.py:24
  123.4 208.0 %reduce-scatter.2.cloned.1.call-done = f32[128,1024]{1,0:T(8,128)} async-done(((f32[4096,1024]{1,0:T(8,128)}), f32[128,1024]{1,0:T(8,128)}) %reduce-scatter.2.cloned.1.call-update) | async-done | bytes 524304 | tf_op jit(solution)/shard_map/reduce_scatter | solution.py:16
  331.4 0.0 copy-done.3
  331.4 2.0 fusion.3
  333.4 0.0 all-gather.2.cloned.1.call-update
  333.4 106.0 %all-gather.2.cloned.1.call-done = bf16[4096,1024]{1,0:T(8,128)(2,1)} async-done(((bf16[128,1024]{1,0:T(8,128)(2,1)}), bf16[4096,1024]{1,0:T(8,128)(2,1)}) %all-gather.2.cloned.1.call-update) | async-done | bytes 8388624 | tf_op jit(solution)/shard_map/all_gather | solution.py:37
  439.4 14.6 %convolution_bitcast_fusion = f32[896,1024]{0,1:T(8,128)} fusion(bf16[4096,1024]{1,0:T(8,128)(2,1)} %all-gather.2.cloned.1.call-done, bf16[4096,896]{1,0:T(8,128)(2,1)} %bitcast.24), kind=kOutput, calls=%fused_computation | convolution fusion | flops 7516192768 | bytes 19398656 | tf_op jit(solution)/shard_map/dot_general | solution.py:38
  454.0 5.0 %copy.11 = f32[896,1024]{1,0:T(8,128)} copy(f32[896,1024]{0,1:T(8,128)} %convolution_bitcast_fusion) | data formatting | bytes 7340032
  (8 shorter events, 0.0 us)
Async XLA Ops:
  7.2 93.6 %copy-start = (bf16[896,1024]{1,0:T(8,128)(2,1)S(1)}, bf16[896,1024]{1,0:T(8,128)(2,1)}, u32[]{:S(2)}) copy-start(bf16[896,1024]{1,0:T(8,128)(2,1)} %param.8) | copy-start | bytes 5505028
  7.2 324.2 %reduce-scatter.2.cloned.1.call-start = ((), (), s32[]{:S(2)}) async-start(), calls=%async_computation.3 | async-start | bytes 17301504 | tf_op jit(solution)/shard_map/reduce_scatter | solution.py:16
  97.9 2.9 copy-start.1
  112.5 0.9 copy-start.2
  112.5 5.2 %copy-start.5 = (s32[16]{0:T(128)S(1)}, s32[16]{0:T(128)}, u32[]{:S(2)}) copy-start(s32[16]{0:T(128)} %param.11) | copy-start | bytes 196
  112.5 5.3 %copy-start.4 = (bf16[1024]{0:T(1024)(128)(2,1)S(1)}, bf16[1024]{0:T(1024)(128)(2,1)}, u32[]{:S(2)}) copy-start(bf16[1024]{0:T(1024)(128)(2,1)} %param.10) | copy-start | bytes 6148
  112.5 218.9 %copy-start.3 = (bf16[128,1024]{1,0:T(8,128)(2,1)S(1)}, bf16[128,1024]{1,0:T(8,128)(2,1)}, u32[]{:S(2)}) copy-start(bf16[128,1024]{1,0:T(8,128)(2,1)} %param.6) | copy-start | bytes 786436
  114.2 9.2 %all-to-all-start.1 = ((bf16[16,8,1024]{2,0,1:T(8,128)(2,1)}), bf16[16,8,1024]{2,0,1:T(8,128)(2,1)S(1)}, u32[]{:S(2)}, u32[]{:S(2)}) async-start(bf16[16,8,1024]{2,0,1:T(8,128)(2,1)} %bitcast.22), calls=%async_computation.2 | async-start | bytes 524288 | tf_op jit(solution)/shard_map/all_to_all | solution.py:24
  117.6 321.8 %all-gather.2.cloned.1.call-start = ((), (), s32[]{:S(2)}) async-start(), calls=%async_computation.4 | async-start | bytes 8650752 | tf_op jit(solution)/shard_map/all_gather | solution.py:37
Sparse Core Ops, SparseCore 0:
  112.7 218.6 reduce-scatter.1
  335.1 104.2 all-gather.1

commit v2 on v0

--- a/solution.py
+++ b/solution.py
@@ -19,7 +19,10 @@
     )
     residual = resid_in.astype(jnp.float32) + mlp_out
     updated = residual.astype(jnp.bfloat16)
-    target_rows = lax.all_to_all(frozen, "shard", split_axis=1, concat_axis=0, tiled=True)
+    target_rows = jnp.concatenate(
+        lax.all_to_all(jnp.stack(jnp.split(frozen, lax.axis_size("shard"), axis=1)), "shard", 0, 0),
+        axis=0,
+    )
     start_row = lax.axis_index("dp") * tok_rows
     seq_ids = (start_row + jnp.arange(tok_rows, dtype=jnp.int32)) // SEQ_LEN
     seq_match = seq_ids[:, None] == jnp.arange(forget_flags.shape[0], dtype=jnp.int32)[None, :]

time: 532 us -> 532 us (level)
  transfers between devices with their start and end apart: 4 -> 4, of which waited for: 4 -> 4; matrix products, arithmetic and copies ran while one was open for 0% -> 1% of each run, Pallas kernels for 0% -> 0%
where the time goes in v2:
time: 532 us
  waiting for transfers between devices  468 us (88%)
  matrix products  29 us (5%)
  between operations  13.8 us (3%)
  local copies, waits for them, and re-layouts  10.9 us (2%)
  starting transfers between devices  7.47 us (1%)
    reduce_scatter x1, waiting for transfers between devices, per_device(): lax.psum_scatter(jnp.dot(whole_hidden, w_down, preferred_element_type=jnp...  199 us
    all_gather x1, waiting for transfers between devices, per_device(): whole_hidden = lax.all_gather(hidden, 'shard', axis=0, tiled=True)  157 us
    all_gather x1, waiting for transfers between devices, per_device(): all_slopes = lax.all_gather(slopes, 'dp', axis=0, tiled=True)  106 us
    dot_general x1, matrix products, per_device(): lax.dot_general(whole_hidden, all_slopes, (((0,), (0,)), ((), ())), prefe...  14.6 us
    dot_general x1, matrix products, per_device(): jnp.dot(whole_hidden, w_down, preferred_element_type=jnp.float32)  14.3 us
  transfers between devices with their start and end apart: 4, of which 4 were waited for; matrix products, arithmetic and copies ran while one was open for 1% of the time, Pallas kernels for 0%

profile of v2, /device:TPU:1, one launch (start us, length us, event | category | flops | bytes accessed | tf_op | source)
XLA Modules:
  0.0 531.7 jit_solution(6417476668491619644)
XLA Ops:
  7.2 0.0 all-gather.3.cloned.1.call-start
  7.2 0.7 all-gather.3.cloned.1.call-update
  7.9 0.0 reduce-scatter.2.cloned.1.call-start
  8.0 156.9 %all-gather.3.cloned.1.call-done = bf16[4096,896]{1,0:T(8,128)(2,1)} async-done(((bf16[512,896]{1,0:T(8,128)(2,1)}), bf16[4096,896]{1,0:T(8,128)(2,1)}) %all-gather.3.cloned.1.call-update) | async-done | bytes 7340048 | tf_op jit(solution)/shard_map/all_gather | solution.py:12
  164.9 14.3 %fusion.5 = f32[4096,1024]{1,0:T(8,128)} fusion(bf16[4096,896]{1,0:T(8,128)(2,1)} %all-gather.3.cloned.1.call-done, bf16[896,1024]{1,0:T(8,128)(2,1)S(1)} %copy-done), kind=kOutput, calls=%fused_computation.24 | convolution fusion | flops 7516192768 | bytes 25952256 | tf_op jit(solution)/shard_map/dot_general | solution.py:15
  179.2 0.0 reduce-scatter.2.cloned.1.call-update
  179.3 0.9 copy-done.1
  180.2 0.6 bitcast_dynamic-update-slice_fusion.7
  180.8 0.6 bitcast_dynamic-update-slice_fusion.6
  181.4 0.6 bitcast_dynamic-update-slice_fusion.5
  182.0 0.6 bitcast_dynamic-update-slice_fusion.4
  182.6 0.6 bitcast_dynamic-update-slice_fusion.3
  183.2 0.6 bitcast_dynamic-update-slice_fusion.2
  183.9 0.6 bitcast_dynamic-update-slice_fusion.1
  184.5 0.6 bitcast_dynamic-update-slice_fusion
  185.1 7.4 %all-to-all-start = ((bf16[8,16,1024]{2,1,0:T(8,128)(2,1)}), bf16[8,16,1024]{2,1,0:T(8,128)(2,1)S(1)}, u32[]{:S(2)}, u32[]{:S(2)}) async-start(bf16[8,16,1024]{2,1,0:T(8,128)(2,1)} %bitcast_dynamic-update-slice_fusion), calls=%async_computation.1 | async-start | bytes 524288 | tf_op jit(solution)/shard_map/all_to_all | solution.py:23
  192.5 0.0 all-gather.5.cloned.1.call-start
  192.5 0.1 select_reduce_fusion
  192.7 5.7 %all-to-all-done = bf16[8,16,1024]{2,1,0:T(8,128)(2,1)S(1)} async-done(((bf16[8,16,1024]{2,1,0:T(8,128)(2,1)}), bf16[8,16,1024]{2,1,0:T(8,128)(2,1)S(1)}, u32[]{:S(2)}, u32[]{:S(2)}) %all-to-all-start) | async-done | bytes 262176 | tf_op jit(solution)/shard_map/all_to_all | solution.py:23
  198.4 199.2 %reduce-scatter.2.cloned.1.call-done = f32[128,1024]{1,0:T(8,128)} async-done(((f32[4096,1024]{1,0:T(8,128)}), f32[128,1024]{1,0:T(8,128)}) %reduce-scatter.2.cloned.1.call-update) | async-done | bytes 524304 | tf_op jit(solution)/shard_map/reduce_scatter | solution.py:14
  397.6 2.0 fusion.3
  399.6 105.9 %all-gather.5.cloned.1.call-done = bf16[4096,1024]{1,0:T(8,128)(2,1)} async-done(((bf16[128,1024]{1,0:T(8,128)(2,1)}), bf16[4096,1024]{1,0:T(8,128)(2,1)}) %all-gather.5.cloned.1.call-update) | async-done | bytes 8388624 | tf_op jit(solution)/shard_map/all_gather | solution.py:38
  505.6 14.6 %convolution_bitcast_fusion = f32[896,1024]{0,1:T(8,128)} fusion(bf16[4096,1024]{1,0:T(8,128)(2,1)} %all-gather.5.cloned.1.call-done, bf16[4096,896]{1,0:T(8,128)(2,1)} %all-gather.3.cloned.1.call-done), kind=kOutput, calls=%fused_computation | convolution fusion | flops 7516192768 | bytes 19398656 | tf_op jit(solution)/shard_map/dot_general | solution.py:39
  520.2 5.0 copy.9
  (14 shorter events, 0.1 us)
Async XLA Ops:
  7.2 157.7 %copy-start = (bf16[896,1024]{1,0:T(8,128)(2,1)S(1)}, bf16[896,1024]{1,0:T(8,128)(2,1)}, u32[]{:S(2)}) copy-start(bf16[896,1024]{1,0:T(8,128)(2,1)} %param.8) | copy-start | bytes 5505028
  7.2 157.7 %all-gather.3.cloned.1.call-start = ((), (), s32[]{:S(2)}) async-start(), calls=%async_computation.2 | async-start | bytes 8257536 | tf_op jit(solution)/shard_map/all_gather | solution.py:12
  7.9 389.7 %reduce-scatter.2.cloned.1.call-start = ((), (), s32[]{:S(2)}) async-start(), calls=%async_computation.3 | async-start | bytes 17301504 | tf_op jit(solution)/shard_map/reduce_scatter | solution.py:14
  179.2 0.9 copy-start.1
  179.2 13.3 %copy-start.4 = (s32[16]{0:T(128)S(1)}, s32[16]{0:T(128)}, u32[]{:S(2)}) copy-start(s32[16]{0:T(128)} %param.11) | copy-start | bytes 196
  179.2 13.4 %copy-start.3 = (bf16[1024]{0:T(1024)(128)(2,1)S(1)}, bf16[1024]{0:T(1024)(128)(2,1)}, u32[]{:S(2)}) copy-start(bf16[1024]{0:T(1024)(128)(2,1)} %param.10) | copy-start | bytes 6148
  179.2 218.4 %copy-start.2 = (bf16[128,1024]{1,0:T(8,128)(2,1)S(1)}, bf16[128,1024]{1,0:T(8,128)(2,1)}, u32[]{:S(2)}) copy-start(bf16[128,1024]{1,0:T(8,128)(2,1)} %param.6) | copy-start | bytes 786436
  185.1 13.3 %all-to-all-start = ((bf16[8,16,1024]{2,1,0:T(8,128)(2,1)}), bf16[8,16,1024]{2,1,0:T(8,128)(2,1)S(1)}, u32[]{:S(2)}, u32[]{:S(2)}) async-start(bf16[8,16,1024]{2,1,0:T(8,128)(2,1)} %bitcast_dynamic-update-slice_fusion), calls=%async_computation.1 | async-start | bytes 524288 | tf_op jit(solution)/shard_map/all_to_all | solution.py:23
  192.5 313.1 %all-gather.5.cloned.1.call-start = ((), (), s32[]{:S(2)}) async-start(), calls=%async_computation.4 | async-start | bytes 8650752 | tf_op jit(solution)/shard_map/all_gather | solution.py:38
Sparse Core Ops, SparseCore 0:
  9.8 155.0 all-gather.2
  179.4 218.1 reduce-scatter.1
  401.3 104.1 all-gather.4
